TPU v7x, 32 devices: a whole 2x2x4 slice. The times are simulated.
32 devices in a mesh: ens: 2 (over x), row: 4 (over z), col: 4 (over y, core).
Axes of the slice: x: 2, y: 2, z: 4, core: 2. Of those that a mesh axis runs over, the one named last changes fastest.
Arguments:
- adjoint: float32 [2, 3, 8, 512, 2048], P('ens', None, 'col', 'row'), may hold values from -6 to 6
- base_flow: float32 [2, 2, 8, 512, 2048], P('ens', None, 'col', 'row'), may hold values from -6 to 6
- stream_first: float32 [16, 128, 128], replicated, may hold values from -0.125 to 0.125
- stream_second: float32 [16, 128, 128], replicated, may hold values from -0.125 to 0.125
- wall_first: float32 [512, 512], replicated, may hold values from -0.25 to 0.25
- wall_second: float32 [512, 512], replicated, may hold values from -0.25 to 0.25
- forcing: float32 [3, 8, 512, 2048], P(None, 'col', 'row'), may hold values from 0.3 to 3
Outputs:
- updated: float32 [2, 3, 8, 512, 2048], P('ens', None, 'col', 'row')
- gradient: float32 [3, 8, 512, 2048], P(None, 'col', 'row')
All inputs are finite; a program needn't handle non-finite values.
Results may differ from a plain program's by a relative error of at most 0.000071.
Values sent between devices are 32-bit elements; how exact they have to be, the bound alone decides.
A program may use at most 384 MiB of HBM per device.

v0:
```python
import functools
import math

import jax
import jax.numpy as jnp
from jax import lax
from jax.experimental import pallas as pl
from jax.experimental.pallas import tpu as pltpu
from jax.sharding import PartitionSpec as P

viscosity = 0.5
step_weight = 0.25
MESH = pl.DeviceIdType.MESH
TILE = 256


def split(v):
    hi = v.astype(jnp.bfloat16)
    return hi, (v - hi.astype(jnp.float32)).astype(jnp.bfloat16)


def turn(re, im, angle):
    c, s = math.cos(angle), math.sin(angle)
    if abs(s) < 1e-12 and c > 0:
        return re, im
    if abs(c) < 1e-12:
        if s < 0:
            return im, (-re if re is not None else None)
        return (-im if im is not None else None), re
    if im is None:
        return re * c, re * s
    return re * c - im * s, re * s + im * c


def plus(a, b):
    if a is None:
        return b
    return a if b is None else a + b


def minus(a, b):
    if b is None:
        return a
    return -b if a is None else a - b


def real_dft(xs):
    n = len(xs)
    if n == 2:
        return [(xs[0] + xs[1], None), (xs[0] - xs[1], None)]
    even, odd = real_dft(xs[0::2]), real_dft(xs[1::2])
    out = [None] * (n // 2 + 1)
    for k in range(n // 4 + 1):
        er, ei = even[k]
        tr, ti = turn(odd[k][0], odd[k][1], -2 * math.pi * k / n)
        out[k] = (plus(er, tr), plus(ei, ti))
        if k != n // 4:
            dr, di = minus(er, tr), minus(ei, ti)
            out[n // 2 - k] = (dr, None if di is None else -di)
    return out


def real_idft(ys):
    n = 2 * (len(ys) - 1)
    if n == 2:
        return [ys[0][0] + ys[1][0], ys[0][0] - ys[1][0]]
    even, odd = [], []
    for k in range(n // 4 + 1):
        ar, ai = ys[k]
        br, bi = ys[n // 2 - k]
        if k == n // 4:
            even.append((ar + ar, None))
            dr, di = None, None if ai is None else ai + ai
        else:
            even.append((ar + br, minus(ai, bi)))
            dr, di = ar - br, plus(ai, bi)
        odd.append(turn(dr, di, 2 * math.pi * k / n))
    for part in (even, odd):
        part[0] = (part[0][0], None)
        part[-1] = (part[-1][0], None)
    e, o = real_idft(even), real_idft(odd)
    out = [None] * n
    out[0::2], out[1::2] = e, o
    return out


def dot_last(a, b):
    return lax.dot_general(a, b, (((1,), (1,)), ((), ())), preferred_element_type=jnp.float32)


def dot(a, b):
    return jnp.dot(a, b, preferred_element_type=jnp.float32)


def kernel(
    units, nz, adj, base, sf_in, ss_in, wf_in, ws_in, forcing, upd_out, grad_out,
    sf, ss, wf, ws,
    own, part, mid, far, flow, flow_in, acc, other, gh, gl, xh, xl, yb, wh, wl, ch, cl,
    s1, r1, s2, r2, s3, r3, s4, r4, s5, r5, sb, rb, la, lb, lf, ou, og, lw,
):
    nc, ny, nx = own.shape
    nb, blk, _ = sf.shape
    half = nb // 2
    nu = len(units)
    e, r = lax.axis_index("ens"), lax.axis_index("row")
    near, across = r ^ 1, r ^ 3
    outer = jnp.logical_or(r == 0, r == 3)
    inner = jnp.logical_not(outer)

    def at(ref, u):
        c, x0, w = units[u]
        return ref.at[c, :, pl.ds(x0, w)]

    def send(src, dst, ssem, rsem, where):
        return pltpu.make_async_remote_copy(
            src_ref=src, dst_ref=dst, send_sem=ssem, recv_sem=rsem,
            device_id=where, device_id_type=MESH)

    def c1(u):
        return send(at(adj, u), at(part, u), s1.at[u], r1.at[u], {"row": near})

    def cb(z):
        return send(base.at[nz + z], flow_in.at[z], sb.at[z], rb.at[z], {"row": near})

    def c2(u):
        return send(at(adj, u), at(mid, u), s2.at[u], r2.at[u], {"row": across})

    def c3(u):
        return send(at(part, u), at(far, u), s3.at[u], r3.at[u], {"row": across})

    def c4(u):
        return send(at(own, u), at(far, u), s4.at[u], r4.at[u], {"row": near})

    def c5(u):
        return send(at(acc, u), at(other, u), s5.at[u], r5.at[u], {"ens": 1 - e})

    def load_adj(c):
        return pltpu.make_async_copy(adj.at[c], own.at[c], la.at[c])

    def load_flow():
        return pltpu.make_async_copy(base, flow, lb)

    def load_forcing(u):
        return pltpu.make_async_copy(at(forcing, u), at(mid, u), lf.at[u])

    def put_upd(u):
        return pltpu.make_async_copy(at(acc, u), at(upd_out, u), ou.at[u])

    def put_grad(u):
        return pltpu.make_async_copy(at(other, u), at(grad_out, u), og.at[u])

    barrier = pltpu.get_barrier_semaphore()
    for where in ({"row": near}, {"row": across}, {"ens": 1 - e}):
        pl.semaphore_signal(barrier, inc=1, device_id=where, device_id_type=MESH)
    pl.semaphore_wait(barrier, 3)

    ahead = min(2, nu)
    reach = min(2, nu - 1)
    lag = min(3, nu)
    order_z = []
    for c, _, _ in units:
        if c % nz not in order_z:
            order_z.append(c % nz)

    @pl.when(outer)
    def _():
        due = {}
        for z in order_z:
            first = min(u for u in range(nu) if units[u][0] % nz == z)
            due.setdefault(min(first + (2 if first == 0 else 0), nu - 1), []).append(z)
        for u in range(nu):
            c1(u).start()
            for z in due.get(u, ()):
                cb(z).start()

    @pl.when(inner)
    def _():
        for u in range(ahead):
            c2(u).start()

    def load_operators():
        pairs = ((sf_in, sf), (ss_in, ss), (wf_in, wf), (ws_in, ws))
        return [pltpu.make_async_copy(a, b, lw.at[i]) for i, (a, b) in enumerate(pairs)]

    for copy in load_operators():
        copy.start()
    for c in range(nc):
        load_adj(c).start()
    load_flow().start()

    for copy in load_operators():
        copy.wait()

    gh[0] = jnp.zeros(gh.shape[1:], gh.dtype)
    gl[0] = jnp.zeros(gl.shape[1:], gl.dtype)

    @pl.loop(0, blk // 16)
    def _(i):
        rows = pl.multiple_of(i * 16, 16)
        for o, (ref, scale) in enumerate(((sf, step_weight), (ss, step_weight * viscosity))):
            xs = [ref[m, pl.ds(rows, 16), :] * (scale / nb) for m in range(nb)]
            fs = real_dft(xs)

            def keep(k, out_half, in_half, v):
                hi, lo = split(v)
                dst = pl.ds(rows + (2 * o + out_half) * blk, 16)
                cols = slice(in_half * blk, (in_half + 1) * blk)
                gh[k, dst, cols] = hi
                gl[k, dst, cols] = lo

            keep(0, 0, 0, fs[0][0])
            keep(0, 1, 1, fs[half][0])
            for k in range(1, half):
                cr, ci = fs[k]
                keep(k, 0, 0, cr)
                keep(k, 0, 1, ci)
                keep(k, 1, 0, -ci)
                keep(k, 1, 1, cr)

    for a, ro in enumerate((r, near)):
        for o, (ref, scale) in enumerate(((wf, step_weight), (ws, step_weight * viscosity))):
            for b, co in enumerate((r, near, across, r ^ 2)):
                v = ref[pl.ds(pl.multiple_of(ro * ny, 128), ny), pl.ds(pl.multiple_of(co * ny, 128), ny)] * scale
                hi, lo = split(v)
                i = 2 * a + o
                wh[i * ny:(i + 1) * ny, b * ny:(b + 1) * ny] = hi
                wl[i * ny:(i + 1) * ny, b * ny:(b + 1) * ny] = lo

    load_flow().wait()

    def stream(c):
        load_adj(c).wait()

        @pl.loop(0, ny // 16)
        def _(i):
            rows = pl.ds(pl.multiple_of(i * 16, 16), 16)
            fs = real_dft([own[c, rows, p * blk:(p + 1) * blk] for p in range(nb)])
            for k in range(half):
                pair = (fs[0][0], fs[half][0]) if k == 0 else fs[k]
                for t in range(2):
                    hi, lo = split(pair[t])
                    at_col = (2 * k + t) * blk
                    xh[rows, at_col:at_col + blk] = hi
                    xl[rows, at_col:at_col + blk] = lo

        @pl.loop(0, half)
        def _(k):
            cols = pl.ds(pl.multiple_of(k * 2 * blk, 128), 2 * blk)
            hi, lo = xh[:, cols], xl[:, cols]
            yb[k] = dot_last(hi, gh[k]) + (dot_last(hi, gl[k]) + dot_last(lo, gh[k]))

        @pl.loop(0, ny // 8)
        def _(i):
            rows = pl.ds(pl.multiple_of(i * 8, 8), 8)
            for o in range(2):
                b0 = 2 * o * blk
                ys = [(yb[0, rows, b0:b0 + blk], None)]
                for k in range(1, half):
                    ys.append((yb[k, rows, b0:b0 + blk], yb[k, rows, b0 + blk:b0 + 2 * blk]))
                ys.append((yb[0, rows, b0 + blk:b0 + 2 * blk], None))
                xs = real_idft(ys)
                for p in range(nb):
                    cols = slice(p * blk, (p + 1) * blk)
                    if o == 0:
                        acc[c, rows, cols] = own[c, rows, cols] + flow[c % nz, rows, cols] * xs[p]
                    else:
                        acc[c, rows, cols] = acc[c, rows, cols] + xs[p]

    def wall(u):
        c, x0, w = units[u]
        z = c % nz

        @pl.loop(0, w // TILE)
        def _(t):
            cols = pl.ds(pl.multiple_of(x0 + t * TILE, 128), TILE)
            for b, ref in enumerate((own, part, mid, far)):
                hi, lo = split(ref[c, :, cols])
                ch[b * ny:(b + 1) * ny, :] = hi
                cl[b * ny:(b + 1) * ny, :] = lo
            hi, lo = ch[...], cl[...]
            y = dot(wh[...], hi) + (dot(wh[...], lo) + dot(wl[...], hi))
            acc[c, :, cols] = acc[c, :, cols] + (y[ny:2 * ny] + flow[nz + z, :, cols] * y[:ny])
            own[c, :, cols] = y[3 * ny:] + flow_in[z, :, cols] * y[2 * ny:3 * ny]

    def add_wall(u):
        c, x0, w = units[u]

        @pl.loop(0, ny // 8)
        def _(i):
            rows = pl.ds(pl.multiple_of(i * 8, 8), 8)
            cols = slice(x0, x0 + w)
            acc[c, rows, cols] = acc[c, rows, cols] + far[c, rows, cols]

    def gradient(u):
        c, x0, w = units[u]
        c5(u).wait_recv()
        load_forcing(u).wait()

        @pl.loop(0, ny // 8)
        def _(i):
            rows = pl.ds(pl.multiple_of(i * 8, 8), 8)
            cols = slice(x0, x0 + w)
            other[c, rows, cols] = mid[c, rows, cols] * (acc[c, rows, cols] + other[c, rows, cols])

        put_grad(u).start()

    done = set()

    turns = []
    for c, _, _ in units:
        if c not in turns:
            turns.append(c)

    def need(i):
        c = turns[min(i, nc - 1)]
        if c not in done:
            done.add(c)
            stream(c)

    def relay(u):
        @pl.when(inner)
        def _():
            c1(u).wait_recv()
            c3(u).start()
            if u + ahead < nu:
                c2(u + ahead).start()

    waited = set()
    need(0)
    for u in range(reach):
        relay(u)
    need(1)
    for u in range(nu):
        if u + reach < nu:
            relay(u + reach)
        c = units[u][0]
        need(turns.index(c))
        need(turns.index(c) + 1)
        z = c % nz
        first = z not in waited
        waited.add(z)

        @pl.when(inner)
        def _():
            if first:
                cb(z).wait_recv()
            c2(u).wait_recv()
            c3(u).wait_recv()
            wall(u)
            c4(u).start()

        @pl.when(outer)
        def _():
            c4(u).wait_recv()
            add_wall(u)

        c5(u).start()
        put_upd(u).start()
        load_forcing(u).start()
        if u >= lag:
            gradient(u - lag)
    for u in range(nu - lag, nu):
        gradient(u)

    @pl.when(outer)
    def _():
        for u in range(nu):
            c1(u).wait_send()
        for z in order_z:
            cb(z).wait_send()

    @pl.when(inner)
    def _():
        for u in range(nu):
            c2(u).wait_send()
            c3(u).wait_send()
            c4(u).wait_send()

    for u in range(nu):
        c5(u).wait_send()
        put_upd(u).wait()
        put_grad(u).wait()


def fused(adjoint, base_flow, stream_first, stream_second, wall_first, wall_second, forcing):
    _, nf, nz, ny, nx = adjoint.shape
    nc = nf * nz
    nb, blk, _ = stream_first.shape
    units = []
    for c in [f * nz + z for z in range(nz) for f in range(nf)]:
        widths = [nx // 2, nx // 2]
        if c == nc - 1:
            widths = [nx // 2, nx // 4, nx // 8, nx // 8]
        x0 = 0
        for w in widths:
            units.append((c, x0, w))
            x0 += w
    nu = len(units)
    f32, bf16 = jnp.float32, jnp.bfloat16
    field = pltpu.VMEM((nc, ny, nx), f32)
    n_ops = 4 * ny
    dma = pltpu.SemaphoreType.DMA
    any_spec = pl.BlockSpec(memory_space=pl.ANY)
    updated, gradient = pl.pallas_call(
        functools.partial(kernel, tuple(units), nz),
        out_shape=(jax.ShapeDtypeStruct((nc, ny, nx), f32), jax.ShapeDtypeStruct((nc, ny, nx), f32)),
        in_specs=[any_spec] * 7,
        out_specs=(any_spec, any_spec),
        scratch_shapes=[pltpu.VMEM(a.shape, f32) for a in (stream_first, stream_second, wall_first, wall_second)] + [
            field, field, field, field,
            pltpu.VMEM((2 * nz, ny, nx), f32), pltpu.VMEM((nz, ny, nx), f32),
            field, field,
            pltpu.VMEM((nb // 2, 4 * blk, 2 * blk), bf16), pltpu.VMEM((nb // 2, 4 * blk, 2 * blk), bf16),
            pltpu.VMEM((ny, nx), bf16), pltpu.VMEM((ny, nx), bf16),
            pltpu.VMEM((nb // 2, ny, 4 * blk), f32),
            pltpu.VMEM((n_ops, 4 * ny), bf16), pltpu.VMEM((n_ops, 4 * ny), bf16),
            pltpu.VMEM((4 * ny, TILE), bf16), pltpu.VMEM((4 * ny, TILE), bf16),
        ] + [dma((nu,))] * 10 + [dma((nz,))] * 2 + [dma((nc,)), dma, dma((nu,)), dma((nu,)), dma((nu,)), dma((4,))],
        compiler_params=pltpu.CompilerParams(
            collective_id=0, has_side_effects=True, vmem_limit_bytes=67043328),
    )(
        adjoint.reshape(nc, ny, nx), base_flow.reshape(-1, ny, nx),
        stream_first, stream_second, wall_first, wall_second, forcing.reshape(nc, ny, nx),
    )
    return updated.reshape(adjoint.shape), gradient.reshape(forcing.shape)


def stream_terms(adj_field, stream_first, stream_second):
    block_count = stream_first.shape[0]
    block_size = stream_first.shape[1]
    blocks_view = adj_field.reshape(-1, block_count, block_size)
    first_sum = jnp.zeros(blocks_view.shape, jnp.float32)
    second_sum = jnp.zeros(blocks_view.shape, jnp.float32)
    for shift_count in range(block_count):
        shifted = jnp.roll(blocks_view, -shift_count, axis=1)
        first_sum = first_sum + jnp.einsum(
            "mpj,ij->mpi", shifted, stream_first[shift_count], precision=lax.Precision.HIGHEST
        )
        second_sum = second_sum + jnp.einsum(
            "mpj,ij->mpi", shifted, stream_second[shift_count], precision=lax.Precision.HIGHEST
        )
    return (first_sum.reshape(adj_field.shape), second_sum.reshape(adj_field.shape))


def local(adjoint, base_flow, stream_first, stream_second, wall_first, wall_second, forcing):
    adj_field = adjoint[0]
    base_speed = base_flow[0]
    x_first, x_second = stream_terms(adj_field, stream_first, stream_second)
    rhs_stream = viscosity * x_second + base_speed[0:1] * x_first
    lines = lax.all_to_all(adj_field, "row", split_axis=3, concat_axis=2, tiled=True)
    y_first = jnp.einsum("ky,fzyx->fzkx", wall_first, lines, precision=lax.Precision.HIGHEST)
    y_second = jnp.einsum("ky,fzyx->fzkx", wall_second, lines, precision=lax.Precision.HIGHEST)
    y_first, y_second = (y_first, y_second)
    y_first, y_second = (
        lax.all_to_all(y_first, "row", split_axis=2, concat_axis=3, tiled=True),
        lax.all_to_all(y_second, "row", split_axis=2, concat_axis=3, tiled=True),
    )
    rhs_wall = viscosity * y_second + base_speed[1:2] * y_first
    updated = adj_field + step_weight * (rhs_stream + rhs_wall)
    summed = lax.psum(updated, "ens")
    gradient = forcing * summed
    return (updated[None], gradient)


def solution(mesh):
    placed = (
        P("ens", None, "col", "row", None),
        P("ens", None, "col", "row", None),
        P(),
        P(),
        P(),
        P(),
        P(None, "col", "row", None),
    )
    small = mesh.shape["row"] == 4 and mesh.shape["ens"] == 2
    return jax.shard_map(
        fused if small else local,
        mesh=mesh,
        in_specs=placed,
        out_specs=(P("ens", None, "col", "row", None), P(None, "col", "row", None)),
        check_vma=False,
    )
```

profile of v0, /device:TPU:0, one launch (start us, length us, event | category | flops | bytes accessed | tf_op | source)
XLA Modules:
  0.0 307.6 jit_solution(11342982432051014288)
XLA Ops:
  0.6 297.8 %shard_map.86 = (f32[6,128,2048]{2,1,0:T(8,128)}, f32[6,128,2048]{2,1,0:T(8,128)}) custom-call(f32[6,128,2048]{2,1,0:T(8,128)} %bitcast.7, f32[4,128,2048]{2,1,0:T(8,128)} %bitcast.9, f32[16,128,128]{2,1,0:T(8,128)} %sf_in.1, f32[16,128,128]{2,1,0:T(8,128)} %ss_in.1, f32[512,512]{1,0:T(8,128)} %wf_in.1, f32[512,512]{1,0:T(8,128)} %ws_in.1, ...), custom_call_target="tpu_custom_call" | custom-call | tf_op jit(solution)/shard_map/pallas_call | solution.py:404
  298.4 0.0 copy-start
  298.4 6.4 %copy.11 = f32[1,3,2,128,2048]{4,3,2,1,0:T(8,128)} copy(f32[1,3,2,128,2048]{4,3,2,1,0:T(8,128)} %bitcast.6) | data formatting | bytes 12582912
  304.9 0.0 copy-done
  304.9 2.7 copy.12
Async XLA Ops:
  298.4 6.4 %copy-start = (f32[6,128,2048]{2,1,0:T(8,128)S(1)}, f32[6,128,2048]{2,1,0:T(8,128)}, u32[]{:S(2)}) copy-start(f32[6,128,2048]{2,1,0:T(8,128)} %get-tuple-element.5) | copy-start | bytes 18874372
where the time goes:
time: 308 us
  Pallas kernels  298 us (97%)
  local copies, waits for them, and re-layouts  9.14 us (3%)
    pallas_call x1, Pallas kernels, fused(): pl.pallas_call(functools.partial(kernel, tuple(units), nz), out_shape=(ja...  298 us
    unnamed x4, local copies, waits for them, and re-layouts  9.14 us

commit v1 on v0

--- a/solution.py
+++ b/solution.py
@@ -156,7 +156,7 @@
 
     ahead = min(2, nu)
     reach = min(2, nu - 1)
-    lag = min(3, nu)
+    lag = min(4, nu)
     order_z = []
     for c, _, _ in units:
         if c % nz not in order_z:
@@ -270,14 +270,16 @@
         c, x0, w = units[u]
         z = c % nz
 
-        @pl.loop(0, w // TILE)
+        tile = min(TILE, w)
+
+        @pl.loop(0, w // tile)
         def _(t):
-            cols = pl.ds(pl.multiple_of(x0 + t * TILE, 128), TILE)
+            cols = pl.ds(pl.multiple_of(x0 + t * tile, 128), tile)
             for b, ref in enumerate((own, part, mid, far)):
                 hi, lo = split(ref[c, :, cols])
-                ch[b * ny:(b + 1) * ny, :] = hi
-                cl[b * ny:(b + 1) * ny, :] = lo
-            hi, lo = ch[...], cl[...]
+                ch[b * ny:(b + 1) * ny, :tile] = hi
+                cl[b * ny:(b + 1) * ny, :tile] = lo
+            hi, lo = ch[:, :tile], cl[:, :tile]
             y = dot(wh[...], hi) + (dot(wh[...], lo) + dot(wl[...], hi))
             acc[c, :, cols] = acc[c, :, cols] + (y[ny:2 * ny] + flow[nz + z, :, cols] * y[:ny])
             own[c, :, cols] = y[3 * ny:] + flow_in[z, :, cols] * y[2 * ny:3 * ny]
@@ -317,22 +319,30 @@
             done.add(c)
             stream(c)
 
+    big = max(u for u in range(nu) if units[u][2] == units[0][2])
+
+    def due_mid(u):
+        return max(min(u + ahead + 1, big + 1), min(u + 2, nu))
+
+    def due_relay(u):
+        return nu if u >= big - 1 else min(u + 1 + reach, nu)
+
     def relay(u):
         @pl.when(inner)
         def _():
             c1(u).wait_recv()
             c3(u).start()
-            if u + ahead < nu:
-                c2(u + ahead).start()
+            for v in range(due_mid(u - 1), due_mid(u)):
+                c2(v).start()
 
     waited = set()
     need(0)
-    for u in range(reach):
+    for u in range(due_relay(-1)):
         relay(u)
     need(1)
     for u in range(nu):
-        if u + reach < nu:
-            relay(u + reach)
+        for v in range(due_relay(u - 1), due_relay(u)):
+            relay(v)
         c = units[u][0]
         need(turns.index(c))
         need(turns.index(c) + 1)
@@ -386,11 +396,14 @@
     _, nf, nz, ny, nx = adjoint.shape
     nc = nf * nz
     nb, blk, _ = stream_first.shape
-    units = []
+    units, turns = [], []
     for c in [f * nz + z for z in range(nz) for f in range(nf)]:
         widths = [nx // 2, nx // 2]
-        if c == nc - 1:
-            widths = [nx // 2, nx // 4, nx // 8, nx // 8]
+        if len(turns) == nc - 2:
+            widths = [nx // 2, nx // 4, nx // 4]
+        if len(turns) == nc - 1:
+            widths = [nx // 4] + [nx // 8] * 5 + [nx // 16] * 2
+        turns.append(c)
         x0 = 0
         for w in widths:
             units.append((c, x0, w))

time: 308 us -> 296 us (0.961)
  Pallas kernels: 298 us -> 286 us
    pallas_call x1, Pallas kernels: 298 us -> 286 us  [fused(): pl.pallas_call(functools.partial(kernel, tuple(units), nz), out_shape=(ja...]
where the time goes in v1:
time: 296 us
  Pallas kernels  286 us (97%)
  local copies, waits for them, and re-layouts  9.14 us (3%)
    pallas_call x1, Pallas kernels, fused(): pl.pallas_call(functools.partial(kernel, tuple(units), nz), out_shape=(ja...  286 us
    unnamed x4, local copies, waits for them, and re-layouts  9.14 us

profile of v1, /device:TPU:0, one launch (start us, length us, event | category | flops | bytes accessed | tf_op | source)
XLA Modules:
  0.0 296.0 jit_solution(15257720101205276515)
XLA Ops:
  0.6 286.2 %shard_map.86 = (f32[6,128,2048]{2,1,0:T(8,128)}, f32[6,128,2048]{2,1,0:T(8,128)}) custom-call(f32[6,128,2048]{2,1,0:T(8,128)} %bitcast.7, f32[4,128,2048]{2,1,0:T(8,128)} %bitcast.9, f32[16,128,128]{2,1,0:T(8,128)} %sf_in.1, f32[16,128,128]{2,1,0:T(8,128)} %ss_in.1, f32[512,512]{1,0:T(8,128)} %wf_in.1, f32[512,512]{1,0:T(8,128)} %ws_in.1, ...), custom_call_target="tpu_custom_call" | custom-call | tf_op jit(solution)/shard_map/pallas_call | solution.py:417
  286.9 0.0 copy-start
  286.9 6.4 %copy.11 = f32[1,3,2,128,2048]{4,3,2,1,0:T(8,128)} copy(f32[1,3,2,128,2048]{4,3,2,1,0:T(8,128)} %bitcast.6) | data formatting | bytes 12582912
  293.3 0.0 copy-done
  293.3 2.7 copy.12
Async XLA Ops:
  286.9 6.4 %copy-start = (f32[6,128,2048]{2,1,0:T(8,128)S(1)}, f32[6,128,2048]{2,1,0:T(8,128)}, u32[]{:S(2)}) copy-start(f32[6,128,2048]{2,1,0:T(8,128)} %get-tuple-element.5) | copy-start | bytes 18874372

commit v2 on v1

--- a/solution.py
+++ b/solution.py
@@ -93,10 +93,10 @@
 
 
 def kernel(
-    units, nz, adj, base, sf_in, ss_in, wf_in, ws_in, forcing, upd_out, grad_out,
+    units, nz, adj, base, sf_in, ss_in, wf_in, ws_in, forcing, acc, other,
     sf, ss, wf, ws,
-    own, part, mid, far, flow, flow_in, acc, other, gh, gl, xh, xl, yb, wh, wl, ch, cl,
-    s1, r1, s2, r2, s3, r3, s4, r4, s5, r5, sb, rb, la, lb, lf, ou, og, lw,
+    own, part, mid, far, flow, flow_in, gh, gl, xh, xl, yb, wh, wl, ch, cl,
+    s1, r1, s2, r2, s3, r3, s4, r4, s5, r5, sb, rb, la, lb, lf, lw,
 ):
     nc, ny, nx = own.shape
     nb, blk, _ = sf.shape
@@ -142,12 +142,6 @@
 
     def load_forcing(u):
         return pltpu.make_async_copy(at(forcing, u), at(mid, u), lf.at[u])
-
-    def put_upd(u):
-        return pltpu.make_async_copy(at(acc, u), at(upd_out, u), ou.at[u])
-
-    def put_grad(u):
-        return pltpu.make_async_copy(at(other, u), at(grad_out, u), og.at[u])
 
     barrier = pltpu.get_barrier_semaphore()
     for where in ({"row": near}, {"row": across}, {"ens": 1 - e}):
@@ -304,8 +298,6 @@
             cols = slice(x0, x0 + w)
             other[c, rows, cols] = mid[c, rows, cols] * (acc[c, rows, cols] + other[c, rows, cols])
 
-        put_grad(u).start()
-
     done = set()
 
     turns = []
@@ -365,7 +357,6 @@
             add_wall(u)
 
         c5(u).start()
-        put_upd(u).start()
         load_forcing(u).start()
         if u >= lag:
             gradient(u - lag)
@@ -388,8 +379,6 @@
 
     for u in range(nu):
         c5(u).wait_send()
-        put_upd(u).wait()
-        put_grad(u).wait()
 
 
 def fused(adjoint, base_flow, stream_first, stream_second, wall_first, wall_second, forcing):
@@ -414,28 +403,48 @@
     n_ops = 4 * ny
     dma = pltpu.SemaphoreType.DMA
     any_spec = pl.BlockSpec(memory_space=pl.ANY)
+    vmem_spec = pl.BlockSpec(memory_space=pltpu.VMEM)
     updated, gradient = pl.pallas_call(
         functools.partial(kernel, tuple(units), nz),
-        out_shape=(jax.ShapeDtypeStruct((nc, ny, nx), f32), jax.ShapeDtypeStruct((nc, ny, nx), f32)),
+        out_shape=(field, field),
         in_specs=[any_spec] * 7,
-        out_specs=(any_spec, any_spec),
+        out_specs=(vmem_spec, vmem_spec),
         scratch_shapes=[pltpu.VMEM(a.shape, f32) for a in (stream_first, stream_second, wall_first, wall_second)] + [
             field, field, field, field,
             pltpu.VMEM((2 * nz, ny, nx), f32), pltpu.VMEM((nz, ny, nx), f32),
-            field, field,
             pltpu.VMEM((nb // 2, 4 * blk, 2 * blk), bf16), pltpu.VMEM((nb // 2, 4 * blk, 2 * blk), bf16),
             pltpu.VMEM((ny, nx), bf16), pltpu.VMEM((ny, nx), bf16),
             pltpu.VMEM((nb // 2, ny, 4 * blk), f32),
             pltpu.VMEM((n_ops, 4 * ny), bf16), pltpu.VMEM((n_ops, 4 * ny), bf16),
             pltpu.VMEM((4 * ny, TILE), bf16), pltpu.VMEM((4 * ny, TILE), bf16),
-        ] + [dma((nu,))] * 10 + [dma((nz,))] * 2 + [dma((nc,)), dma, dma((nu,)), dma((nu,)), dma((nu,)), dma((4,))],
+        ] + [dma((nu,))] * 10 + [dma((nz,))] * 2 + [dma((nc,)), dma, dma((nu,)), dma((4,))],
         compiler_params=pltpu.CompilerParams(
-            collective_id=0, has_side_effects=True, vmem_limit_bytes=67043328),
+            collective_id=0, has_side_effects=True, vmem_limit_bytes=48 << 20),
     )(
         adjoint.reshape(nc, ny, nx), base_flow.reshape(-1, ny, nx),
         stream_first, stream_second, wall_first, wall_second, forcing.reshape(nc, ny, nx),
     )
+    hbm = jax.ShapeDtypeStruct((nc, ny, nx), f32)
+    updated, gradient = pl.pallas_call(
+        put,
+        out_shape=(hbm, hbm),
+        in_specs=[vmem_spec, vmem_spec],
+        out_specs=(any_spec, any_spec),
+        scratch_shapes=[dma((2, nc))],
+        compiler_params=pltpu.CompilerParams(vmem_limit_bytes=1 << 20),
+    )(updated, gradient)
     return updated.reshape(adjoint.shape), gradient.reshape(forcing.shape)
+
+
+def put(updated, gradient, upd_out, grad_out, sem):
+    copies = []
+    for i, (src, dst) in enumerate(((updated, upd_out), (gradient, grad_out))):
+        for c in range(src.shape[0]):
+            copies.append(pltpu.make_async_copy(src.at[c], dst.at[c], sem.at[i, c]))
+    for copy in copies:
+        copy.start()
+    for copy in copies:
+        copy.wait()
 
 
 def stream_terms(adj_field, stream_first, stream_second):

time: 296 us -> 291 us (0.983)
  local copies, waits for them, and re-layouts: 9.14 us -> 0 us
  Pallas kernels: 286 us -> 290 us
    unnamed x4 -> x0, local copies, waits for them, and re-layouts: 9.14 us -> none
    pallas_call x1 -> x2, Pallas kernels: 286 us -> 290 us  [the longest x1 285 us: fused(): pl.pallas_call(functools.partial(kernel, tuple(units), nz), out_shape=(fi...]
where the time goes in v2:
time: 291 us
  Pallas kernels  290 us (100%)
    pallas_call x1, Pallas kernels, fused(): pl.pallas_call(functools.partial(kernel, tuple(units), nz), out_shape=(fi...  285 us

profile of v2, /device:TPU:0, one launch (start us, length us, event | category | flops | bytes accessed | tf_op | source)
XLA Modules:
  0.0 290.7 jit_solution(13007047714519405908)
XLA Ops:
  0.6 285.4 %shard_map.86 = (f32[6,128,2048]{2,1,0:T(8,128)S(1)}, f32[6,128,2048]{2,1,0:T(8,128)S(1)}) custom-call(f32[6,128,2048]{2,1,0:T(8,128)} %bitcast.5, f32[4,128,2048]{2,1,0:T(8,128)} %bitcast.7, f32[16,128,128]{2,1,0:T(8,128)} %sf_in.1, f32[16,128,128]{2,1,0:T(8,128)} %ss_in.1, f32[512,512]{1,0:T(8,128)} %wf_in.1, f32[512,512]{1,0:T(8,128)} %ws_in.1, ...), custom_call_target="tpu_custom_call" | custom-call | tf_op jit(solution)/shard_map/pallas_call | solution.py:407
  286.0 4.7 %shard_map.87 = (f32[6,128,2048]{2,1,0:T(8,128)}, f32[6,128,2048]{2,1,0:T(8,128)}) custom-call(f32[6,128,2048]{2,1,0:T(8,128)S(1)} %get-tuple-element.6.updated, f32[6,128,2048]{2,1,0:T(8,128)S(1)} %get-tuple-element.7.gradient), custom_call_target="tpu_custom_call" | custom-call | tf_op jit(solution)/shard_map/pallas_call | solution.py:428
